TPU v7x, 128 devices: a whole 4x4x4 slice. The times are simulated.
128 devices in a mesh: grp: 8 (over y, z_lo), tp: 16 (over z_hi, x, core).
Axes of the slice: x: 4, y: 4, z: 4 (z_hi: 2, z_lo: 2; z = z_hi * 2 + z_lo), core: 2. Of those that a mesh axis runs over, the one named last changes fastest.
Arguments:
- features: bfloat16 [2048, 49152], P('grp', 'tp'), may hold values from -24 to 24
- weight: bfloat16 [49152, 8192], P('tp', 'grp'), may hold values from -0.049804688 to 0.049804688
- norm_gain: float32 [8192], P('grp'), may hold values from 0.1 to 1.9
- target: bfloat16 [2048, 8192], P(None, 'grp'), may hold values from -6 to 6
- counts: int32 [256], replicated, may hold values from 1 to 8
Outputs:
- weight_grad: bfloat16 [49152, 8192], P('tp', 'grp')
- draft_loss: float32 [], replicated
All inputs are finite; a program needn't handle non-finite values.
Results may differ from a plain program's by a relative error of at most 0.0085.
Values may be sent and summed in bfloat16 or wider, within the bound.
A program may use at most 128 MiB of HBM per device.

v0:
```python
import jax
import jax.numpy as jnp
from jax import lax
from jax.sharding import PartitionSpec as P

DOUT = 8192
SPEC = 8
epsilon = 1e-06


def row_mask(counts, row_start, row_count):
    row_index = row_start + jnp.arange(row_count, dtype=jnp.int32)
    owner = jnp.take(counts, row_index // SPEC)
    return (row_index % SPEC < owner).astype(jnp.float32)[:, None]


def backward_rows(hidden, target_rows, row_live, norm_gain, accepted):
    gain_row = norm_gain[None, :]
    squares = lax.psum(jnp.sum(hidden * hidden, axis=1), "grp")
    inverse_rms = lax.rsqrt(squares / DOUT + epsilon)[:, None]
    normed = hidden * inverse_rms * gain_row
    deviation = normed - target_rows
    residual = row_live * deviation / accepted
    coupling = lax.psum(jnp.sum(gain_row * residual * hidden, axis=1), "grp")[:, None]
    act_grad = (
        inverse_rms * gain_row * residual - hidden * inverse_rms**3 * coupling / DOUT
    ).astype(jnp.bfloat16)
    partial_loss = 0.5 * jnp.sum(residual * deviation)
    return (act_grad, partial_loss)


def shards(features, weight, norm_gain, target, counts):
    gathered = lax.all_gather(features, "grp", axis=0, tiled=True)
    total_rows = gathered.shape[0]
    accepted = jnp.sum(counts).astype(jnp.float32)
    rows_here = total_rows // lax.axis_size("tp")
    row_start = lax.axis_index("tp") * rows_here
    hidden = lax.psum_scatter(
        jnp.dot(gathered, weight, preferred_element_type=jnp.float32).astype(jnp.bfloat16),
        "tp",
        scatter_dimension=0,
        tiled=True,
    ).astype(jnp.float32)
    target_rows = lax.dynamic_slice_in_dim(target, row_start, rows_here, 0).astype(jnp.float32)
    row_live = row_mask(counts, row_start, rows_here)
    act_grad, partial_loss = backward_rows(hidden, target_rows, row_live, norm_gain, accepted)
    all_grad = lax.all_gather(act_grad, "tp", axis=0, tiled=True)
    draft_loss = lax.psum(partial_loss, ("grp", "tp"))
    weight_grad = lax.dot_general(
        gathered, all_grad, (((0,), (0,)), ((), ())), preferred_element_type=jnp.float32
    ).astype(jnp.bfloat16)
    return (weight_grad, draft_loss)


def solution(mesh):
    placed = (P("grp", "tp"), P("tp", "grp"), P("grp"), P(None, "grp"), P())
    return jax.shard_map(
        shards, mesh=mesh, in_specs=placed, out_specs=(P("tp", "grp"), P()), check_vma=False
    )
```

profile of v0, /device:TPU:1, one launch (start us, length us, event | category | flops | bytes accessed | tf_op | source)
XLA Modules:
  0.0 507.1 jit_solution(5090543502613461760)
XLA Ops:
  7.2 0.0 all-gather.3.cloned.1.call-start
  7.2 0.7 all-gather.3.cloned.1.call-update
  7.9 0.0 copy-start
  7.9 0.0 copy-start.1
  7.9 0.0 reduce-scatter.2.cloned.1.call-start
  8.0 251.7 %all-gather.3.cloned.1.call-done = bf16[2048,3072]{1,0:T(8,128)(2,1)} async-done(((bf16[256,3072]{1,0:T(8,128)(2,1)}), bf16[2048,3072]{1,0:T(8,128)(2,1)}) %all-gather.3.cloned.1.call-update) | async-done | bytes 12582928 | tf_op jit(solution)/shard_map/all_gather | solution.py:33
  259.7 18.8 %convolution_convert_fusion = bf16[2048,1024]{1,0:T(8,128)(2,1)} fusion(bf16[2048,3072]{1,0:T(8,128)(2,1)} %all-gather.3.cloned.1.call-done, bf16[3072,1024]{1,0:T(8,128)(2,1)} %param.6), kind=kOutput, calls=%fused_computation.2 | convolution fusion | flops 12886999040 | bytes 23068672 | tf_op jit(solution)/shard_map/dot_general | solution.py:39
  278.5 0.0 reduce-scatter.2.cloned.1.call-update
  278.5 0.0 all-gather.5.cloned.1.call-start
  278.5 0.0 copy-done
  278.5 0.6 reduce_sum.37
  279.9 1.3 gather_fusion
  281.2 77.8 %reduce-scatter.2.cloned.1.call-done = bf16[128,1024]{1,0:T(8,128)(2,1)} async-done(((bf16[2048,1024]{1,0:T(8,128)(2,1)}), bf16[128,1024]{1,0:T(8,128)(2,1)}) %reduce-scatter.2.cloned.1.call-update) | async-done | bytes 262160 | tf_op jit(solution)/shard_map/reduce_scatter | solution.py:38
  359.0 1.1 fusion
  360.1 15.3 %psum.21 = f32[128]{0:T(128)S(1)} all-reduce(f32[128]{0:T(128)S(1)} %fusion), channel_id=1, replica_groups=mesh['grp'=8,'tp'=16] {'grp'}, use_global_device_ids=true, to_apply=%region_2.3 | all-reduce | flops 128 | bytes 1024 | tf_op jit(solution)/shard_map/psum | solution.py:19
  375.4 0.0 copy-done.1
  375.4 2.0 multiply_reduce_fusion
  377.4 12.5 %psum.22 = f32[128]{0:T(128)S(1)} all-reduce(f32[128]{0:T(128)S(1)} %get-tuple-element.7), channel_id=1, replica_groups=mesh['grp'=8,'tp'=16] {'grp'}, use_global_device_ids=true, to_apply=%region_5.6 | all-reduce | flops 128 | bytes 1024 | tf_op jit(solution)/shard_map/psum | solution.py:24
  389.9 2.0 fusion.6
  391.9 0.0 all-gather.5.cloned.1.call-update
  392.6 80.8 %psum.23 = f32[]{:T(128)} all-reduce(f32[]{:T(128)S(6)} %mul_shard_map.3), channel_id=1, replica_groups=mesh['grp'=8,'tp'=16] {'grp','tp'}, use_global_device_ids=true, to_apply=%region_7.8 | all-reduce | flops 1 | bytes 8 | tf_op jit(solution)/shard_map/psum | solution.py:48
  473.4 0.0 all-gather.5.cloned.1.call-done
  473.4 18.6 %convert_bitcast_fusion = bf16[3072,1024]{0,1:T(8,128)(2,1)} fusion(bf16[2048,1024]{1,0:T(8,128)(2,1)} %all-gather.5.cloned.1.call-done, bf16[2048,3072]{1,0:T(8,128)(2,1)} %all-gather.3.cloned.1.call-done), kind=kOutput, calls=%fused_computation.1 | convolution fusion | flops 12888047616 | bytes 23068672 | tf_op jit(solution)/shard_map/dot_general | solution.py:49
  492.0 8.6 %copy.8 = bf16[3072,1024]{1,0:T(8,128)(2,1)} copy(bf16[3072,1024]{0,1:T(8,128)(2,1)} %convert_bitcast_fusion) | data formatting | bytes 12582912
  (4 shorter events, 0.0 us)
Async XLA Ops:
  7.2 252.5 %all-gather.3.cloned.1.call-start = ((), (), s32[]{:S(2)}) async-start(), calls=%async_computation.1 | async-start | bytes 14155776 | tf_op jit(solution)/shard_map/all_gather | solution.py:33
  7.9 270.6 %copy-start = (s32[256]{0:T(256)S(1)}, s32[256]{0:T(256)}, u32[]{:S(2)}) copy-start(s32[256]{0:T(256)} %param.9) | copy-start | bytes 3076
  7.9 367.5 %copy-start.1 = (f32[1024]{0:T(1024)S(1)}, f32[1024]{0:T(1024)}, u32[]{:S(2)}) copy-start(f32[1024]{0:T(1024)} %param.7) | copy-start | bytes 12292
  7.9 351.1 %reduce-scatter.2.cloned.1.call-start = ((), (), s32[]{:S(2)}) async-start(), calls=%async_computation.2 | async-start | bytes 4456448 | tf_op jit(solution)/shard_map/reduce_scatter | solution.py:38
  278.5 194.9 %all-gather.5.cloned.1.call-start = ((), (), s32[]{:S(2)}) async-start(), calls=%async_computation.3 | async-start | bytes 4456448 | tf_op jit(solution)/shard_map/all_gather | solution.py:47
Sparse Core Ops, SparseCore 0:
  9.6 250.0 all-gather.2
  278.6 80.3 reduce-scatter.1
  392.1 62.8 all-gather.4
where the time goes:
time: 508 us; the launch traced here: 507 us
  waiting for transfers between devices  330 us (65%)
  blocking collectives  109 us (21%)
  matrix products  37.4 us (7%)
  between operations  15.1 us (3%)
  local copies, waits for them, and re-layouts  9.89 us (2%)
  other arithmetic  5.84 us (1%)
    all_gather x1, waiting for transfers between devices, shards(): gathered = lax.all_gather(features, 'grp', axis=0, tiled=True)  252 us
    psum x1, blocking collectives, shards(): draft_loss = lax.psum(partial_loss, ('grp', 'tp'))  80.8 us
    reduce_scatter x1, waiting for transfers between devices, shards(): lax.psum_scatter(jnp.dot(gathered, weight, preferred_element_type=jnp.flo...  77.8 us
    dot_general x1, matrix products, shards(): jnp.dot(gathered, weight, preferred_element_type=jnp.float32)  18.8 us
    dot_general x1, matrix products, shards(): lax.dot_general(gathered, all_grad, (((0,), (0,)), ((), ())), preferred_e...  18.6 us
    psum x1, blocking collectives, backward_rows(): squares = lax.psum(jnp.sum(hidden * hidden, axis=1), 'grp')  15.3 us
    psum x1, blocking collectives, backward_rows(): lax.psum(jnp.sum(gain_row * residual * hidden, axis=1), 'grp')[:, None]  12.5 us
  transfers between devices with their start and end apart: 3, of which 2 were waited for; matrix products, arithmetic and copies ran while one was open for 0% of the time, Pallas kernels for 0%

commit v1 on v0

--- a/solution.py
+++ b/solution.py
@@ -30,7 +30,8 @@
 
 
 def shards(features, weight, norm_gain, target, counts):
-    gathered = lax.all_gather(features, "grp", axis=0, tiled=True)
+    repeated = jnp.stack([features] * lax.axis_size("grp"))
+    gathered = jnp.concatenate(lax.all_to_all(repeated, "grp", 0, 0), axis=0)
     total_rows = gathered.shape[0]
     accepted = jnp.sum(counts).astype(jnp.float32)
     rows_here = total_rows // lax.axis_size("tp")

time: 508 us -> 411 us (0.81)
  waiting for transfers between devices: 330 us -> 78.4 us
  blocking collectives: 109 us -> 255 us
  local copies, waits for them, and re-layouts: 9.89 us -> 22 us
    all_gather x1 -> x0, waiting for transfers between devices: 252 us -> none  [shards(): gathered = lax.all_gather(features, 'grp', axis=0, tiled=True)]
    all_to_all x0 -> x1, blocking collectives: none -> 146 us  [shards(): gathered = jnp.concatenate(lax.all_to_all(repeated, 'grp', 0, 0), axis=0)]
    another operation x0 -> x1, local copies, waits for them, and re-layouts: none -> 7.58 us  [shards(): repeated = jnp.stack([features] * lax.axis_size('grp'))]
    unnamed x5 -> x9, local copies, waits for them, and re-layouts: 8.62 us -> 13.2 us
  transfers between devices with their start and end apart: 3 -> 2, of which waited for: 2 -> 1; matrix products, arithmetic and copies ran while one was open for 0% -> 0% of each run, Pallas kernels for 0% -> 0%
where the time goes in v1:
time: 411 us; the launch traced here: 410 us
  blocking collectives  255 us (62%)
  waiting for transfers between devices  78.4 us (19%)
  matrix products  33.4 us (8%)
  local copies, waits for them, and re-layouts  22 us (5%)
  between operations  15.4 us (4%)
  other arithmetic  5.84 us (1%)
    all_to_all x1, blocking collectives, shards(): gathered = jnp.concatenate(lax.all_to_all(repeated, 'grp', 0, 0), axis=0)  146 us
    psum x1, blocking collectives, shards(): draft_loss = lax.psum(partial_loss, ('grp', 'tp'))  80.7 us
    reduce_scatter x1, waiting for transfers between devices, shards(): lax.psum_scatter(jnp.dot(gathered, weight, preferred_element_type=jnp.flo...  78.4 us
    dot_general x1, matrix products, shards(): lax.dot_general(gathered, all_grad, (((0,), (0,)), ((), ())), preferred_e...  18.6 us
    psum x1, blocking collectives, backward_rows(): squares = lax.psum(jnp.sum(hidden * hidden, axis=1), 'grp')  15.3 us
    dot_general x1, matrix products, shards(): jnp.dot(gathered, weight, preferred_element_type=jnp.float32)  14.8 us
    unnamed x9, local copies, waits for them, and re-layouts  13.2 us
    psum x1, blocking collectives, backward_rows(): lax.psum(jnp.sum(gain_row * residual * hidden, axis=1), 'grp')[:, None]  12.5 us
  transfers between devices with their start and end apart: 2, of which 1 were waited for; matrix products, arithmetic and copies ran while one was open for 0% of the time, Pallas kernels for 0%

profile of v1, /device:TPU:1, one launch (start us, length us, event | category | flops | bytes accessed | tf_op | source)
XLA Modules:
  0.0 410.1 jit_solution(1600271808743552085)
XLA Ops:
  7.2 0.0 reduce-scatter.2.cloned.1.call-start
  7.2 7.6 %stack.2 = bf16[8,256,3072]{2,1,0:T(8,128)(2,1)} broadcast(bf16[256,3072]{1,0:T(8,128)(2,1)} %param.5), dimensions={1,2} | broadcast | bytes 14155776 | tf_op jit(solution)/shard_map/stack | solution.py:33
  14.8 0.0 copy-start.3
  14.8 146.4 %all_to_all.5 = bf16[8,256,3072]{2,1,0:T(8,128)(2,1)S(1)} all-to-all(bf16[8,256,3072]{2,1,0:T(8,128)(2,1)} %stack.2), channel_id=1, replica_groups=mesh['grp'=8,'tp'=16] {'grp'}, dimensions={0} | all-to-all | bytes 25165824 | tf_op jit(solution)/shard_map/all_to_all | solution.py:34
  161.2 0.0 copy-start.1
  161.2 4.6 %copy-done.1 = bf16[8,256,3072]{2,1,0:T(8,128)(2,1)} copy-done((bf16[8,256,3072]{2,1,0:T(8,128)(2,1)}, bf16[8,256,3072]{2,1,0:T(8,128)(2,1)S(1)}, u32[]{:S(2)}) %copy-start.1) | copy-done | bytes 12582936
  165.8 0.0 copy-done.3
  165.8 0.0 copy-start
  165.8 0.0 copy-start.2
  165.8 14.8 %convolution_convert_fusion = bf16[2048,1024]{1,0:T(8,128)(2,1)} fusion(bf16[2048,3072]{1,0:T(8,128)(2,1)S(1)} %bitcast.9, bf16[3072,1024]{1,0:T(8,128)(2,1)S(1)} %copy-done.3), kind=kOutput, calls=%fused_computation.2 | convolution fusion | flops 12886999040 | bytes 23068672 | tf_op jit(solution)/shard_map/dot_general | solution.py:40
  180.5 0.0 reduce-scatter.2.cloned.1.call-update
  180.6 0.0 all-gather.2.cloned.1.call-start
  180.6 0.0 copy-done
  180.6 0.6 reduce_sum.37
  181.9 1.3 gather_fusion
  183.2 78.4 %reduce-scatter.2.cloned.1.call-done = bf16[128,1024]{1,0:T(8,128)(2,1)} async-done(((bf16[2048,1024]{1,0:T(8,128)(2,1)}), bf16[128,1024]{1,0:T(8,128)(2,1)}) %reduce-scatter.2.cloned.1.call-update) | async-done | bytes 262160 | tf_op jit(solution)/shard_map/reduce_scatter | solution.py:39
  261.6 1.1 fusion
  262.7 15.3 %psum.21 = f32[128]{0:T(128)S(1)} all-reduce(f32[128]{0:T(128)S(1)} %fusion), channel_id=1, replica_groups=mesh['grp'=8,'tp'=16] {'grp'}, use_global_device_ids=true, to_apply=%region_2.3 | all-reduce | flops 128 | bytes 1024 | tf_op jit(solution)/shard_map/psum | solution.py:19
  278.0 0.0 copy-done.2
  278.1 2.0 multiply_reduce_fusion
  280.1 12.5 %psum.22 = f32[128]{0:T(128)S(1)} all-reduce(f32[128]{0:T(128)S(1)} %get-tuple-element.7), channel_id=1, replica_groups=mesh['grp'=8,'tp'=16] {'grp'}, use_global_device_ids=true, to_apply=%region_5.6 | all-reduce | flops 128 | bytes 1024 | tf_op jit(solution)/shard_map/psum | solution.py:24
  292.5 2.0 fusion.6
  294.6 0.0 all-gather.2.cloned.1.call-update
  295.3 80.7 %psum.23 = f32[]{:T(128)} all-reduce(f32[]{:T(128)S(6)} %mul_shard_map.3), channel_id=1, replica_groups=mesh['grp'=8,'tp'=16] {'grp','tp'}, use_global_device_ids=true, to_apply=%region_7.8 | all-reduce | flops 1 | bytes 8 | tf_op jit(solution)/shard_map/psum | solution.py:49
  376.0 0.0 all-gather.2.cloned.1.call-done
  376.0 18.6 %convert_bitcast_fusion = bf16[3072,1024]{0,1:T(8,128)(2,1)} fusion(bf16[2048,1024]{1,0:T(8,128)(2,1)} %all-gather.2.cloned.1.call-done, bf16[2048,3072]{1,0:T(8,128)(2,1)} %bitcast.10), kind=kOutput, calls=%fused_computation.1 | convolution fusion | flops 12888047616 | bytes 23068672 | tf_op jit(solution)/shard_map/dot_general | solution.py:50
  394.6 8.6 %copy.8 = bf16[3072,1024]{1,0:T(8,128)(2,1)} copy(bf16[3072,1024]{0,1:T(8,128)(2,1)} %convert_bitcast_fusion) | data formatting | bytes 12582912
  (4 shorter events, 0.0 us)
Async XLA Ops:
  7.2 254.4 %reduce-scatter.2.cloned.1.call-start = ((), (), s32[]{:S(2)}) async-start(), calls=%async_computation.2 | async-start | bytes 4456448 | tf_op jit(solution)/shard_map/reduce_scatter | solution.py:39
  14.8 151.0 %copy-start.3 = (bf16[3072,1024]{1,0:T(8,128)(2,1)S(1)}, bf16[3072,1024]{1,0:T(8,128)(2,1)}, u32[]{:S(2)}) copy-start(bf16[3072,1024]{1,0:T(8,128)(2,1)} %param.6) | copy-start | bytes 18874372
  161.2 4.6 %copy-start.1 = (bf16[8,256,3072]{2,1,0:T(8,128)(2,1)}, bf16[8,256,3072]{2,1,0:T(8,128)(2,1)S(1)}, u32[]{:S(2)}) copy-start(bf16[8,256,3072]{2,1,0:T(8,128)(2,1)S(1)} %all_to_all.5) | copy-start | bytes 37748740
  165.8 14.8 %copy-start = (s32[256]{0:T(256)S(1)}, s32[256]{0:T(256)}, u32[]{:S(2)}) copy-start(s32[256]{0:T(256)} %param.9) | copy-start | bytes 3076
  165.8 112.3 %copy-start.2 = (f32[1024]{0:T(1024)S(1)}, f32[1024]{0:T(1024)}, u32[]{:S(2)}) copy-start(f32[1024]{0:T(1024)} %param.7) | copy-start | bytes 12292
  180.6 195.4 %all-gather.2.cloned.1.call-start = ((), (), s32[]{:S(2)}) async-start(), calls=%async_computation.3 | async-start | bytes 4456448 | tf_op jit(solution)/shard_map/all_gather | solution.py:48
Sparse Core Ops, SparseCore 0:
  180.7 80.8 reduce-scatter.1
  294.7 62.8 all-gather.1
